TPU v7x, 256 devices: a whole 4x4x8 slice. The times are simulated.
256 devices in a mesh: ctx: 8 (over z_hi, core), vocab: 32 (over x, y, z_lo).
Axes of the slice: x: 4, y: 4, z: 8 (z_hi: 4, z_lo: 2; z = z_hi * 2 + z_lo), core: 2. Of those that a mesh axis runs over, the one named last changes fastest.
Arguments:
- hidden: bfloat16 [512, 2, 7168], P('ctx', None, 'vocab'), may hold values from -30 to 30
- head: bfloat16 [7168, 65536], P('ctx', 'vocab'), may hold values from -0.15 to 0.15
- targets: int32 [512, 2], P('ctx'), may hold values from 0 to 65535
- loss_weight: float32 [512, 2], P('ctx'), may hold values from 16 to 256
Outputs:
- token_loss: float32 [512, 2], P('ctx')
- grad_hidden: bfloat16 [512, 2, 7168], P('ctx', None, 'vocab')
All inputs are finite; a program needn't handle non-finite values.
Results may differ from a plain program's by a relative error of at most 0.0046.
Values may be sent and summed in bfloat16 or wider, within the bound.
A program may use at most 64 MiB of HBM per device.

v0:
```python
import jax
import jax.numpy as jnp
from jax import lax
from jax.sharding import PartitionSpec as P


def sent_to_all(x, axis):
    copies = jnp.broadcast_to(x, (lax.axis_size(axis), *x.shape))
    return lax.all_to_all(copies, axis, split_axis=0, concat_axis=0, tiled=True)


def gathered_once(x, axis):
    leaves = jax.tree.leaves(x)
    order = sorted(range(len(leaves)), key=lambda k: -leaves[k].size)
    width = (1, *leaves[order[0]].shape)[-1]
    lines = [
        jnp.pad(leaves[k].reshape(-1), (0, -leaves[k].size % width)).reshape(-1, width)
        for k in order
    ]
    both, at, found = (sent_to_all(jnp.concatenate(lines), axis), 0, {})
    for k, line in zip(order, lines):
        slab = both[:, at : at + len(line)].reshape(len(both), -1)
        found[k] = slab[:, : leaves[k].size].reshape(-1, *leaves[k].shape)
        at += len(line)
    numbers = iter(range(len(leaves)))
    return jax.tree.map(lambda _: found[next(numbers)], x)


def combined_pairwise(pieces, combine):
    while len(jax.tree.leaves(pieces)[0]) > 1:
        pieces = jax.vmap(combine)(
            *(jax.tree.map(lambda part: part[side::2], pieces) for side in (0, 1))
        )
    return jax.tree.map(lambda part: part[0], pieces)


def joined_all(x, axis, combine):
    pieces = gathered_once(x, axis)
    return combined_pairwise(pieces, combine)


def cut_along(x, dim, size):
    lengths = x.shape
    pieces = x.reshape(*lengths[:dim], size, lengths[dim] // size, *lengths[dim + 1 :])
    return jnp.moveaxis(pieces, dim, 0)


def summed_on_arrival(x, axis, dim):
    pieces = cut_along(x, dim, lax.axis_size(axis))
    arrived = lax.all_to_all(pieces, axis, split_axis=0, concat_axis=0, tiled=True)
    return arrived.sum(axis=0)


def combine_stats(first, second):
    first_max, first_sum, first_target = first
    second_max, second_sum, second_target = second
    joined = jnp.maximum(first_max, second_max)
    total = first_sum * jnp.exp(first_max - joined) + second_sum * jnp.exp(second_max - joined)
    return (joined, total, first_target + second_target)


def body(hidden, head, targets, loss_weight):
    group_rows = hidden.shape[0]
    depth_count = hidden.shape[1]
    flat_count = group_rows * depth_count
    ctx_count = lax.axis_size("ctx")
    vocab_count = lax.axis_size("vocab")
    vocab_index = lax.axis_index("vocab")
    vocab_local = head.shape[1]
    flat_hidden = hidden.reshape(flat_count, hidden.shape[2])
    flat_targets = targets.reshape(flat_count)
    flat_weights = loss_weight.reshape(flat_count)
    whole_width = lax.all_gather(flat_hidden, "vocab", axis=1, tiled=True)
    width_slab = lax.all_to_all(whole_width, "ctx", split_axis=1, concat_axis=0, tiled=True)
    logits = lax.psum_scatter(
        jnp.dot(width_slab, head, preferred_element_type=jnp.float32),
        "ctx",
        scatter_dimension=0,
        tiled=True,
    )
    columns = vocab_index * vocab_local + lax.broadcasted_iota(jnp.int32, logits.shape, 1)
    target_hit = columns == flat_targets[:, None]
    local_max = jnp.max(logits, axis=1)
    local_target = jnp.sum(jnp.where(target_hit, logits, 0.0), axis=1)
    local_sum = jnp.sum(jnp.exp(logits - local_max[:, None]), axis=1)
    row_max, sum_exp, target_logit = joined_all(
        (local_max, local_sum, local_target), "vocab", combine_stats
    )
    flat_loss = jnp.log(sum_exp) + row_max - target_logit
    token_loss = flat_loss.reshape(group_rows, depth_count)
    probabilities = jnp.exp(logits - row_max[:, None]) / sum_exp[:, None]
    dlogits = (flat_weights[:, None] * (probabilities - target_hit.astype(jnp.float32))).astype(
        jnp.bfloat16
    )
    grad_slab = lax.dot_general(
        lax.all_gather(dlogits, "ctx", axis=0, tiled=True),
        head,
        (((1,), (1,)), ((), ())),
        preferred_element_type=jnp.float32,
    )
    share_rows = flat_count // vocab_count
    slab_width = grad_slab.shape[1]
    blocks = grad_slab.reshape(ctx_count, vocab_count, share_rows, slab_width)
    reduced = summed_on_arrival(blocks, "vocab", 1).astype(jnp.bfloat16)
    landed = lax.all_to_all(
        lax.all_to_all(reduced, "ctx", split_axis=0, concat_axis=3, tiled=True),
        "vocab",
        split_axis=3,
        concat_axis=1,
        tiled=True,
    )
    grad_out = landed.reshape(group_rows, depth_count, landed.shape[3])
    return (token_loss, grad_out)


def solution(mesh):
    return jax.shard_map(
        body,
        mesh=mesh,
        in_specs=(P("ctx", None, "vocab"), P("ctx", "vocab"), P("ctx", None), P("ctx", None)),
        out_specs=(P("ctx", None), P("ctx", None, "vocab")),
        check_vma=False,
    )
```

profile of v0, /device:TPU:1, one launch (start us, length us, event | category | flops | bytes accessed | tf_op | source)
XLA Modules:
  0.0 565.0 jit_solution(5996300982655620662)
XLA Ops:
  7.2 0.9 reshape.54
  8.1 0.7 copy.29
  8.9 141.3 %all-gather.3.cloned.1.call-done = bf16[128,7168]{0,1:T(8,128)(2,1)} async-done(((bf16[128,224]{0,1:T(8,128)(2,1)}), bf16[128,7168]{0,1:T(8,128)(2,1)}) %all-gather.3.cloned.1.call-update) | async-done | bytes 1835024 | tf_op jit(solution)/shard_map/all_gather | solution.py:73
  150.2 72.8 %all_to_all.62 = bf16[128,8,896]{0,2,1:T(8,128)(2,1)S(1)} all-to-all(bf16[128,8,896]{0,2,1:T(8,128)(2,1)} %bitcast.42), channel_id=1, replica_groups=mesh['ctx'=8,'vocab'=32] {'ctx'}, dimensions={1} | all-to-all | bytes 3670016 | tf_op jit(solution)/shard_map/all_to_all | solution.py:74
  222.9 2.7 copy.30
  225.6 10.3 %fusion.6 = f32[1024,2048]{1,0:T(8,128)} fusion(bf16[1024,896]{1,0:T(8,128)(2,1)} %bitcast.43, bf16[896,2048]{1,0:T(8,128)(2,1)} %param.5), kind=kOutput, calls=%fused_computation.20 | convolution fusion | flops 3758096384 | bytes 13893632 | tf_op jit(solution)/shard_map/dot_general | solution.py:76
  236.0 0.6 copy-done
  236.9 88.8 %reduce-scatter.2.cloned.1.call-done = f32[128,2048]{1,0:T(8,128)} async-done(((f32[1024,2048]{1,0:T(8,128)}), f32[128,2048]{1,0:T(8,128)}) %reduce-scatter.2.cloned.1.call-update) | async-done | bytes 1048592 | tf_op jit(solution)/shard_map/reduce_scatter | solution.py:75
  325.7 1.4 reduce_max.9
  327.0 1.6 exponential_reduce_fusion
  328.6 0.6 broadcast_in_dim.9
  329.3 8.1 %all-to-all-start.1 = ((f32[32,3,128]{2,1,0:T(4,128)}), f32[32,3,128]{2,1,0:T(4,128)S(1)}, u32[]{:S(2)}, u32[]{:S(2)}) async-start(f32[32,3,128]{2,1,0:T(4,128)} %broadcast_in_dim.9), calls=%async_computation.2 | async-start | bytes 131072 | tf_op jit(solution)/shard_map/all_to_all | solution.py:9
  337.6 0.1 mul.54
  337.7 6.9 %all-to-all-done.1 = f32[32,3,128]{2,1,0:T(4,128)S(1)} async-done(((f32[32,3,128]{2,1,0:T(4,128)}), f32[32,3,128]{2,1,0:T(4,128)S(1)}, u32[]{:S(2)}, u32[]{:S(2)}) %all-to-all-start.1) | async-done | bytes 49184 | tf_op jit(solution)/shard_map/all_to_all | solution.py:9
  345.2 2.4 fusion.3
  347.7 51.8 %all-gather.5.cloned.1.call-done = bf16[1024,2048]{1,0:T(8,128)(2,1)} async-done(((bf16[128,2048]{1,0:T(8,128)(2,1)}), bf16[1024,2048]{1,0:T(8,128)(2,1)}) %all-gather.5.cloned.1.call-update) | async-done | bytes 4194320 | tf_op jit(solution)/shard_map/all_gather | solution.py:96
  399.5 9.7 %fusion.7 = f32[1024,896]{1,0:T(8,128)} fusion(bf16[1024,2048]{1,0:T(8,128)(2,1)} %all-gather.5.cloned.1.call-done, bf16[896,2048]{1,0:T(8,128)(2,1)} %param.5), kind=kOutput, calls=%fused_computation.21 | convolution fusion | flops 3758096384 | bytes 11534336 | tf_op jit(solution)/shard_map/dot_general | solution.py:95
  409.2 5.0 reshape_reshape.3
  414.2 3.1 copy.46
  417.2 52.6 %all_to_all.63 = f32[32,8,1,4,896]{4,3,1,2,0:T(4,128)} all-to-all(f32[32,8,1,4,896]{4,3,1,2,0:T(4,128)S(1)} %bitcast.38), channel_id=1, replica_groups=mesh['ctx'=8,'vocab'=32] {'vocab'}, dimensions={0} | all-to-all | bytes 7340032 | tf_op jit(solution)/shard_map/all_to_all | solution.py:50
  469.9 2.7 reduce_sum.29
  472.5 12.3 %all_to_all.64 = bf16[8,1,4,896]{3,2,1,0:T(4,128)(2,1)S(1)} all-to-all(bf16[8,1,4,896]{3,2,1,0:T(4,128)(2,1)S(1)} %bitcast.45), channel_id=1, replica_groups=mesh['ctx'=8,'vocab'=32] {'ctx'}, dimensions={0} | all-to-all | bytes 114688 | tf_op jit(solution)/shard_map/all_to_all | solution.py:106
  484.8 6.0 %copy.38 = bf16[1,1,4,7168]{2,1,0,3:T(2,128)(2,1)} copy(bf16[1,1,4,7168]{3,2,1,0:T(4,128)(2,1)S(1)} %bitcast.46) | data formatting | bytes 114688 | tf_op jit(solution)/shard_map/all_to_all | solution.py:106
  490.8 0.5 broadcast.6
  491.3 39.8 %reduce.5 = bf16[7168,4]{1,0:T(8,128)(2,1)S(1)} reduce(bf16[7168,1,1,4]{3,2,1,0:T(2,128)(2,1)} %bitcast.40, bf16[]{:T(256)} %broadcast.6), dimensions={1,2}, to_apply=%bitcast.31.reduce_sub_computation | reduce | bytes 114690
  531.1 2.5 reshape.69
  533.6 3.9 all-to-all-start.4
  537.6 0.6 copy.41
  538.2 6.5 %all-to-all-done.4 = bf16[32,2,448]{2,1,0:T(2,128)(2,1)S(1)} async-done(((bf16[32,2,448]{2,1,0:T(2,128)(2,1)}), bf16[32,2,448]{2,1,0:T(2,128)(2,1)S(1)}, u32[]{:S(2)}, u32[]{:S(2)}) %all-to-all-start.4) | async-done | bytes 57376 | tf_op jit(solution)/shard_map/all_to_all | solution.py:105
  544.7 5.7 %reshape.70 = bf16[7168,1,1,4]{3,2,1,0:T(2,128)(2,1)} reshape(bf16[32,2,448]{2,1,0:T(2,128)(2,1)S(1)} %all-to-all-done.4) | data formatting | bytes 114688
  550.5 7.1 %copy.39 = bf16[1,1,4,7168]{3,2,1,0:T(4,128)(2,1)S(1)} copy(bf16[1,1,4,7168]{2,1,0,3:T(2,128)(2,1)} %bitcast.39) | data formatting | bytes 114688 | tf_op jit(solution)/shard_map/all_to_all | solution.py:105
  557.8 0.7 reshape.61
  (51 shorter events, 1.3 us)
Async XLA Ops:
  7.2 143.0 %all-gather.3.cloned.1.call-start = ((), (), s32[]{:S(2)}) async-start(), calls=%async_computation.6 | async-start | bytes 1892352 | tf_op jit(solution)/shard_map/all_gather | solution.py:73
  8.9 316.8 %reduce-scatter.2.cloned.1.call-start = ((), (), s32[]{:S(2)}) async-start(), calls=%async_computation.7 | async-start | bytes 9437184 | tf_op jit(solution)/shard_map/reduce_scatter | solution.py:75
  235.9 0.7 copy-start
  236.0 101.5 %copy-start.1 = (f32[64,2]{0,1:T(2,128)S(1)}, f32[64,2]{0,1:T(2,128)}, u32[]{:S(2)}) copy-start(f32[64,2]{0,1:T(2,128)} %param.7) | copy-start | bytes 1540
  329.3 15.3 %all-to-all-start.1 = ((f32[32,3,128]{2,1,0:T(4,128)}), f32[32,3,128]{2,1,0:T(4,128)S(1)}, u32[]{:S(2)}, u32[]{:S(2)}) async-start(f32[32,3,128]{2,1,0:T(4,128)} %broadcast_in_dim.9), calls=%async_computation.2 | async-start | bytes 131072 | tf_op jit(solution)/shard_map/all_to_all | solution.py:9
  337.4 62.1 %all-gather.5.cloned.1.call-start = ((), (), s32[]{:S(2)}) async-start(), calls=%async_computation.8 | async-start | bytes 4718592 | tf_op jit(solution)/shard_map/all_gather | solution.py:96
  533.6 11.1 %all-to-all-start.4 = ((bf16[32,2,448]{2,1,0:T(2,128)(2,1)}), bf16[32,2,448]{2,1,0:T(2,128)(2,1)S(1)}, u32[]{:S(2)}, u32[]{:S(2)}) async-start(bf16[32,2,448]{2,1,0:T(2,128)(2,1)} %reshape.69), calls=%async_computation.5 | async-start | bytes 131072 | tf_op jit(solution)/shard_map/all_to_all | solution.py:105
Sparse Core Ops, SparseCore 0:
  10.3 139.7 all-gather.2
  236.1 89.5 reduce-scatter.1
  347.8 51.6 all-gather.4
where the time goes:
time: 566 us; the launch traced here: 565 us
  waiting for transfers between devices  295 us (52%)
  blocking collectives  138 us (24%)
  other arithmetic  47.9 us (8%)
  local copies, waits for them, and re-layouts  38.1 us (7%)
  matrix products  20 us (4%)
  between operations  13.9 us (2%)
  starting transfers between devices  12.1 us (2%)
    all_gather x1, waiting for transfers between devices, body(): whole_width = lax.all_gather(flat_hidden, 'vocab', axis=1, tiled=True)  141 us
    reduce_scatter x1, waiting for transfers between devices, body(): lax.psum_scatter(jnp.dot(width_slab, head, preferred_element_type=jnp.flo...  88.8 us
    all_to_all x1, blocking collectives, body(): lax.all_to_all(whole_width, 'ctx', split_axis=1, concat_axis=0, tiled=True)  72.8 us
    all_to_all x1, blocking collectives, summed_on_arrival(): lax.all_to_all(pieces, axis, split_axis=0, concat_axis=0, tiled=True)  52.6 us
    all_gather x1, waiting for transfers between devices, body(): lax.all_gather(dlogits, 'ctx', axis=0, tiled=True)  51.8 us
    unnamed x1, other arithmetic  39.8 us
    all_to_all x1, blocking collectives, body(): lax.all_to_all(reduced, 'ctx', split_axis=0, concat_axis=3, tiled=True)  12.3 us
  transfers between devices with their start and end apart: 5, of which 5 were waited for; matrix products, arithmetic and copies ran while one was open for 0% of the time, Pallas kernels for 0%

commit v1 on v0

--- a/solution.py
+++ b/solution.py
@@ -70,7 +70,9 @@
     flat_hidden = hidden.reshape(flat_count, hidden.shape[2])
     flat_targets = targets.reshape(flat_count)
     flat_weights = loss_weight.reshape(flat_count)
-    whole_width = lax.all_gather(flat_hidden, "vocab", axis=1, tiled=True)
+    whole_width = jnp.concatenate(
+        lax.all_to_all(jnp.stack([flat_hidden] * lax.axis_size("vocab")), "vocab", 0, 0), axis=1
+    )
     width_slab = lax.all_to_all(whole_width, "ctx", split_axis=1, concat_axis=0, tiled=True)
     logits = lax.psum_scatter(
         jnp.dot(width_slab, head, preferred_element_type=jnp.float32),

time: 566 us -> 439 us (0.78)
  waiting for transfers between devices: 295 us -> 153 us
  blocking collectives: 138 us -> 153 us
    all_gather x1 -> x0, waiting for transfers between devices: 141 us -> none  [body(): whole_width = lax.all_gather(flat_hidden, 'vocab', axis=1, tiled=True)]
    all_to_all x0 -> x1, blocking collectives: none -> 34.2 us  [body(): lax.all_to_all(jnp.stack([flat_hidden] * lax.axis_size('vocab')), 'vocab'...]
    all_to_all x1, blocking collectives: 72.8 us -> 54.1 us  [body(): lax.all_to_all(whole_width, 'ctx', split_axis=1, concat_axis=0, tiled=True)]
  transfers between devices with their start and end apart: 5 -> 4, of which waited for: 5 -> 4; matrix products, arithmetic and copies ran while one was open for 0% -> 0% of each run, Pallas kernels for 0% -> 0%
where the time goes in v1:
time: 439 us
  blocking collectives  153 us (35%)
  waiting for transfers between devices  153 us (35%)
  other arithmetic  47.9 us (11%)
  local copies, waits for them, and re-layouts  37.7 us (9%)
  matrix products  20 us (5%)
  between operations  14.2 us (3%)
  starting transfers between devices  12.2 us (3%)
    reduce_scatter x1, waiting for transfers between devices, body(): lax.psum_scatter(jnp.dot(width_slab, head, preferred_element_type=jnp.flo...  87.8 us
    all_to_all x1, blocking collectives, body(): lax.all_to_all(whole_width, 'ctx', split_axis=1, concat_axis=0, tiled=True)  54.1 us
    all_to_all x1, blocking collectives, summed_on_arrival(): lax.all_to_all(pieces, axis, split_axis=0, concat_axis=0, tiled=True)  52.6 us
    all_gather x1, waiting for transfers between devices, body(): lax.all_gather(dlogits, 'ctx', axis=0, tiled=True)  51.8 us
    unnamed x1, other arithmetic  39.8 us
    all_to_all x1, blocking collectives, body(): lax.all_to_all(jnp.stack([flat_hidden] * lax.axis_size('vocab')), 'vocab'...  34.2 us
    all_to_all x1, blocking collectives, body(): lax.all_to_all(reduced, 'ctx', split_axis=0, concat_axis=3, tiled=True)  12.5 us
    dot_general x1, matrix products, body(): jnp.dot(width_slab, head, preferred_element_type=jnp.float32)  10.3 us
  transfers between devices with their start and end apart: 4, of which 4 were waited for; matrix products, arithmetic and copies ran while one was open for 0% of the time, Pallas kernels for 0%

profile of v1, /device:TPU:1, one launch (start us, length us, event | category | flops | bytes accessed | tf_op | source)
XLA Modules:
  0.0 438.5 jit_solution(13208148441567297351)
XLA Ops:
  7.2 0.9 stack_reshape.2
  8.2 0.2 stack.3
  8.5 34.2 %all_to_all.67 = bf16[32,128,224]{1,2,0:T(8,128)(2,1)S(1)} all-to-all(bf16[32,128,224]{1,2,0:T(8,128)(2,1)S(1)} %stack.3), channel_id=1, replica_groups=mesh['ctx'=8,'vocab'=32] {'vocab'}, dimensions={0} | all-to-all | bytes 3670016 | tf_op jit(solution)/shard_map/all_to_all | solution.py:74
  42.6 54.1 %all_to_all.68 = bf16[128,8,896]{0,2,1:T(8,128)(2,1)S(1)} all-to-all(bf16[128,8,896]{0,2,1:T(8,128)(2,1)S(1)} %bitcast.43), channel_id=1, replica_groups=mesh['ctx'=8,'vocab'=32] {'ctx'}, dimensions={1} | all-to-all | bytes 3670016 | tf_op jit(solution)/shard_map/all_to_all | solution.py:76
  96.7 2.7 copy.33
  99.4 10.3 %fusion.6 = f32[1024,2048]{1,0:T(8,128)} fusion(bf16[1024,896]{1,0:T(8,128)(2,1)} %bitcast.45, bf16[896,2048]{1,0:T(8,128)(2,1)} %param.5), kind=kOutput, calls=%fused_computation.20 | convolution fusion | flops 3758096384 | bytes 13893632 | tf_op jit(solution)/shard_map/dot_general | solution.py:78
  109.8 0.6 copy-done
  110.7 87.8 %reduce-scatter.2.cloned.1.call-done = f32[128,2048]{1,0:T(8,128)} async-done(((f32[1024,2048]{1,0:T(8,128)}), f32[128,2048]{1,0:T(8,128)}) %reduce-scatter.2.cloned.1.call-update) | async-done | bytes 1048592 | tf_op jit(solution)/shard_map/reduce_scatter | solution.py:77
  198.5 1.4 reduce_max.9
  199.9 1.6 exponential_reduce_fusion
  201.5 0.6 broadcast_in_dim.9
  202.1 8.3 %all-to-all-start.2 = ((f32[32,3,128]{2,1,0:T(4,128)}), f32[32,3,128]{2,1,0:T(4,128)S(1)}, u32[]{:S(2)}, u32[]{:S(2)}) async-start(f32[32,3,128]{2,1,0:T(4,128)} %broadcast_in_dim.9), calls=%async_computation.3 | async-start | bytes 131072 | tf_op jit(solution)/shard_map/all_to_all | solution.py:9
  210.6 0.1 mul.54
  210.7 6.9 %all-to-all-done.2 = f32[32,3,128]{2,1,0:T(4,128)S(1)} async-done(((f32[32,3,128]{2,1,0:T(4,128)}), f32[32,3,128]{2,1,0:T(4,128)S(1)}, u32[]{:S(2)}, u32[]{:S(2)}) %all-to-all-start.2) | async-done | bytes 49184 | tf_op jit(solution)/shard_map/all_to_all | solution.py:9
  218.2 2.4 fusion.3
  220.7 51.8 %all-gather.2.cloned.1.call-done = bf16[1024,2048]{1,0:T(8,128)(2,1)} async-done(((bf16[128,2048]{1,0:T(8,128)(2,1)}), bf16[1024,2048]{1,0:T(8,128)(2,1)}) %all-gather.2.cloned.1.call-update) | async-done | bytes 4194320 | tf_op jit(solution)/shard_map/all_gather | solution.py:98
  272.4 9.7 %fusion.7 = f32[1024,896]{1,0:T(8,128)} fusion(bf16[1024,2048]{1,0:T(8,128)(2,1)} %all-gather.2.cloned.1.call-done, bf16[896,2048]{1,0:T(8,128)(2,1)} %param.5), kind=kOutput, calls=%fused_computation.21 | convolution fusion | flops 3758096384 | bytes 11534336 | tf_op jit(solution)/shard_map/dot_general | solution.py:97
  282.1 5.0 %reshape_reshape.3 = f32[8,32,1,4,896]{4,3,1,0,2:T(4,128)} reshape(f32[1024,896]{1,0:T(8,128)} %fusion.7) | data formatting | bytes 7340032 | tf_op jit(solution)/shard_map/reshape;reshape | solution.py:44
  287.1 3.1 copy.49
  290.2 52.6 %all_to_all.69 = f32[32,8,1,4,896]{4,3,1,2,0:T(4,128)} all-to-all(f32[32,8,1,4,896]{4,3,1,2,0:T(4,128)S(1)} %bitcast.40), channel_id=1, replica_groups=mesh['ctx'=8,'vocab'=32] {'vocab'}, dimensions={0} | all-to-all | bytes 7340032 | tf_op jit(solution)/shard_map/all_to_all | solution.py:50
  342.8 2.7 reduce_sum.29
  345.5 12.5 %all_to_all.70 = bf16[8,1,4,896]{3,2,1,0:T(4,128)(2,1)S(1)} all-to-all(bf16[8,1,4,896]{3,2,1,0:T(4,128)(2,1)S(1)} %bitcast.47), channel_id=1, replica_groups=mesh['ctx'=8,'vocab'=32] {'ctx'}, dimensions={0} | all-to-all | bytes 114688 | tf_op jit(solution)/shard_map/all_to_all | solution.py:108
  358.0 6.0 %copy.41 = bf16[1,1,4,7168]{2,1,0,3:T(2,128)(2,1)} copy(bf16[1,1,4,7168]{3,2,1,0:T(4,128)(2,1)S(1)} %bitcast.48) | data formatting | bytes 114688 | tf_op jit(solution)/shard_map/all_to_all | solution.py:108
  364.0 0.5 broadcast.7
  364.5 39.8 %reduce.5 = bf16[7168,4]{1,0:T(8,128)(2,1)S(1)} reduce(bf16[7168,1,1,4]{3,2,1,0:T(2,128)(2,1)} %bitcast.42, bf16[]{:T(256)} %broadcast.7), dimensions={1,2}, to_apply=%bitcast.33.reduce_sub_computation | reduce | bytes 114690
  404.3 2.5 reshape.73
  406.8 3.9 all-to-all-start.5
  410.8 0.6 copy.44
  411.4 6.5 %all-to-all-done.5 = bf16[32,2,448]{2,1,0:T(2,128)(2,1)S(1)} async-done(((bf16[32,2,448]{2,1,0:T(2,128)(2,1)}), bf16[32,2,448]{2,1,0:T(2,128)(2,1)S(1)}, u32[]{:S(2)}, u32[]{:S(2)}) %all-to-all-start.5) | async-done | bytes 57376 | tf_op jit(solution)/shard_map/all_to_all | solution.py:107
  417.9 5.8 %reshape.74 = bf16[7168,1,1,4]{3,2,1,0:T(2,128)(2,1)} reshape(bf16[32,2,448]{2,1,0:T(2,128)(2,1)S(1)} %all-to-all-done.5) | data formatting | bytes 114688
  423.7 7.1 %copy.42 = bf16[1,1,4,7168]{3,2,1,0:T(4,128)(2,1)S(1)} copy(bf16[1,1,4,7168]{2,1,0,3:T(2,128)(2,1)} %bitcast.41) | data formatting | bytes 114688 | tf_op jit(solution)/shard_map/all_to_all | solution.py:107
  431.0 0.7 reshape.65
  (50 shorter events, 1.4 us)
Async XLA Ops:
  7.2 191.4 %reduce-scatter.2.cloned.1.call-start = ((), (), s32[]{:S(2)}) async-start(), calls=%async_computation.7 | async-start | bytes 9437184 | tf_op jit(solution)/shard_map/reduce_scatter | solution.py:77
  109.8 0.7 copy-start
  109.8 100.7 %copy-start.1 = (f32[64,2]{0,1:T(2,128)S(1)}, f32[64,2]{0,1:T(2,128)}, u32[]{:S(2)}) copy-start(f32[64,2]{0,1:T(2,128)} %param.7) | copy-start | bytes 1540
  202.1 15.5 %all-to-all-start.2 = ((f32[32,3,128]{2,1,0:T(4,128)}), f32[32,3,128]{2,1,0:T(4,128)S(1)}, u32[]{:S(2)}, u32[]{:S(2)}) async-start(f32[32,3,128]{2,1,0:T(4,128)} %broadcast_in_dim.9), calls=%async_computation.3 | async-start | bytes 131072 | tf_op jit(solution)/shard_map/all_to_all | solution.py:9
  210.4 62.0 %all-gather.2.cloned.1.call-start = ((), (), s32[]{:S(2)}) async-start(), calls=%async_computation.8 | async-start | bytes 4718592 | tf_op jit(solution)/shard_map/all_gather | solution.py:98
  406.8 11.1 %all-to-all-start.5 = ((bf16[32,2,448]{2,1,0:T(2,128)(2,1)}), bf16[32,2,448]{2,1,0:T(2,128)(2,1)S(1)}, u32[]{:S(2)}, u32[]{:S(2)}) async-start(bf16[32,2,448]{2,1,0:T(2,128)(2,1)} %reshape.73), calls=%async_computation.6 | async-start | bytes 131072 | tf_op jit(solution)/shard_map/all_to_all | solution.py:107
Sparse Core Ops, SparseCore 0:
  109.9 88.5 reduce-scatter.1
  220.8 51.5 all-gather.1
